TPU v7x, 512 devices: a whole 4x8x8 slice. The times are simulated.
512 devices in a mesh: leaf: 128 (over y, z, core), sub: 4 (over x).
Axes of the slice: x: 4, y: 8, z: 8, core: 2. Of those that a mesh axis runs over, the one named last changes fastest.
Arguments:
- field: float32 [64, 524288], P(None, ('leaf', 'sub')), may hold values from -6 to 6
- coords: float32 [3, 524288], P(None, ('leaf', 'sub')), may hold values from -6 to 6
- basis: float32 [2048, 64, 256], P(('leaf', 'sub')), may hold values from -0.375 to 0.375
- up_transfer: float32 [2048, 64, 64], P(('leaf', 'sub')), may hold values from -0.1875 to 0.1875
- down_transfer: float32 [2048, 64, 64], P(('leaf', 'sub')), may hold values from -0.75 to 0.75
- couplings: float32 [16384, 64, 64], P(('leaf', 'sub')), may hold values from -0.25 to 0.25
- top_coupling: float32 [128, 128, 64, 64], P('leaf', None, 'sub'), may hold values from -0.25 to 0.25
- send_leaf: int32 [128, 4, 128, 1], P('leaf', 'sub'), may hold values from 0 to 3
- list_slot: int32 [2048, 8], P(('leaf', 'sub')), may hold values from 0 to 127, as said below
- list_block: int32 [2048, 8], P(('leaf', 'sub')), may hold values from 0 to 31
Outputs:
- result: float32 [64, 524288], P(None, ('leaf', 'sub'))
Inputs may be any that keep to these rules, and one draw needn't show every extreme that they name: send_leaf[e, s, d, c] is the leaf, among the 4 of device (e, s), whose skeleton fills slot c of what that device sends to device (d, s). `list_slot`: a list entry q names slot q % 1 from the device q // 1 of the leaf axis with the same sub index; where a device's 4 * 8 list entries are at least 128, every slot is named by some entry of that device, else the device's entries are all different. `list_block`: a list entry names one of the 32 coupling blocks of the leaf's own device.
All inputs are finite; a program needn't handle non-finite values.
Results may differ from a plain program's by a relative error of at most 0.0001.
Values sent between devices are 32-bit elements; how exact they have to be, the bound alone decides.
A program may use at most 64 MiB of HBM per device.

v0:
```python
import math
import jax
import jax.numpy as jnp
from jax import lax
from jax.sharding import PartitionSpec as P

highest = lax.Precision.HIGHEST


def extended(block, sides, width):
    for axis, dim in sides:
        count = lax.axis_size(axis)
        forward = [(i, i + 1) for i in range(count - 1)]
        backward = [(target, source) for source, target in forward]
        low = lax.ppermute(
            lax.slice_in_dim(block, block.shape[dim] - width, None, axis=dim), axis, forward
        )
        high = lax.ppermute(lax.slice_in_dim(block, 0, width, axis=dim), axis, backward)
        block = jnp.concatenate([low, block, high], axis=dim)
    return block


def kernel_block(source_points, target_points, leaf_size):
    dist = jnp.zeros((source_points.shape[1], target_points.shape[1]), jnp.float32)
    for component in range(3):
        gap = source_points[component][:, None] - target_points[component][None, :]
        dist = dist + gap * gap
    return jnp.exp(-0.5 * dist) * (1.0 / math.sqrt(leaf_size))


def add_top(rows, coupling_rows):
    return jnp.einsum("epr,erq->pq", rows, coupling_rows, precision=highest)


def far_terms(incoming, list_slot, chosen, rows, rank):
    gathered = incoming.reshape(-1, rows, rank)[list_slot]
    return jnp.einsum("lkpr,lkrq->lpq", gathered, chosen, precision=highest)


def one_product(
    field,
    coords,
    basis,
    up_transfer,
    down_transfer,
    couplings,
    top_coupling,
    send_leaf,
    list_slot,
    list_block,
):
    rhs_count = field.shape[0]
    leaf_count = basis.shape[0]
    rank = basis.shape[1]
    leaf_size = basis.shape[2]
    stacked = jnp.concatenate([field, coords], 0)
    padded = extended(stacked, ((("leaf", "sub"), 1),), leaf_size)
    leaf_field = field.reshape(rhs_count, leaf_count, leaf_size)
    skeleton = jnp.einsum("pla,lra->lpr", leaf_field, basis, precision=highest)
    outgoing = skeleton[send_leaf.reshape(-1)]
    slot_total = outgoing.shape[0]
    chosen = couplings[list_block]
    incoming = lax.all_to_all(
        outgoing.reshape(slot_total, rhs_count * rank),
        "leaf",
        split_axis=0,
        concat_axis=0,
        tiled=True,
    )
    far = far_terms(incoming, list_slot, chosen, rhs_count, rank)

    def near_leaf(position):
        window = lax.dynamic_slice_in_dim(padded, position * leaf_size, 3 * leaf_size, 1)
        own_points = lax.dynamic_slice_in_dim(
            padded[rhs_count:], (position + 1) * leaf_size, leaf_size, 1
        )
        kernels = kernel_block(window[rhs_count:], own_points, leaf_size)
        return jnp.dot(
            window[:rhs_count], kernels, precision=highest, preferred_element_type=jnp.float32
        )

    near = lax.map(near_leaf, jnp.arange(leaf_count, dtype=jnp.int32))
    parent_part = jnp.einsum("lpr,lrq->pq", skeleton, up_transfer, precision=highest)
    quarter = top_coupling.shape[2]
    coupling_rows = top_coupling[0]
    parent = lax.psum(parent_part, "sub")
    row_start = lax.axis_index("sub") * quarter
    rows = lax.dynamic_slice_in_dim(
        lax.all_gather(parent[None], "leaf", axis=0, tiled=True), row_start, quarter, 2
    )
    top_partial = add_top(rows, coupling_rows)
    top_term = lax.psum(top_partial, "sub")
    coef = far + jnp.einsum("pr,lrq->lpq", top_term, down_transfer, precision=highest)
    total = near + jnp.einsum("lpr,lra->lpa", coef, basis, precision=highest)
    return total.transpose(1, 0, 2).reshape(rhs_count, leaf_count * leaf_size)


def local(
    field,
    coords,
    basis,
    up_transfer,
    down_transfer,
    couplings,
    top_coupling,
    send_leaf,
    list_slot,
    list_block,
):
    current = field
    for repeat in range(2):
        current = one_product(
            current,
            coords,
            basis,
            up_transfer,
            down_transfer,
            couplings,
            top_coupling,
            send_leaf,
            list_slot,
            list_block,
        )
    return current


def solution(mesh):
    in_specs = (
        P(None, ("leaf", "sub")),
        P(None, ("leaf", "sub")),
        P(("leaf", "sub"), None, None),
        P(("leaf", "sub"), None, None),
        P(("leaf", "sub"), None, None),
        P(("leaf", "sub"), None, None),
        P("leaf", None, "sub", None),
        P("leaf", "sub", None, None),
        P(("leaf", "sub"), None),
        P(("leaf", "sub"), None),
    )
    out_specs = P(None, ("leaf", "sub"))
    return jax.shard_map(local, mesh=mesh, in_specs=in_specs, out_specs=out_specs, check_vma=False)
```

profile of v0, /device:TPU:16, one launch (start us, length us, event | category | flops | bytes accessed | tf_op | source)
XLA Modules:
  0.0 379.2 jit_solution(1473924243727374704)
XLA Ops:
  9.2 17.7 %psum.28 = f32[1,64,64]{2,1,0:T(8,128)} all-reduce(f32[1,64,64]{2,1,0:T(8,128)S(1)} %convolution_bitcast_fusion.9), channel_id=1, replica_groups=mesh['leaf'=128,'sub'=4] {'sub'}, use_global_device_ids=true, to_apply=%region_2.3 | all-reduce | flops 4096 | bytes 32768 | tf_op jit(solution)/shard_map/psum | solution.py:86
  28.2 2.8 gather_fusion
  31.0 3.8 copy.27
  34.8 4.1 %copy.28 = f32[128,1,4096]{2,1,0:T(1,128)} copy(f32[128,1,4096]{0,2,1:T(8,128)S(1)} %bitcast.122) | data formatting | bytes 4194304 | tf_op jit(solution)/shard_map/all_to_all | solution.py:63
  38.9 17.8 %all-to-all-start = ((f32[128,1,4096]{2,1,0:T(1,128)}), f32[128,1,4096]{2,1,0:T(1,128)}, u32[]{:S(2)}, u32[]{:S(2)}) async-start(f32[128,1,4096]{2,1,0:T(1,128)} %copy.28), calls=%async_computation | async-start | bytes 4194304 | tf_op jit(solution)/shard_map/all_to_all | solution.py:63
  56.8 1.9 collective-permute-start
  58.8 7.9 %collective-permute-start.1 = (f32[67,256]{1,0:T(8,128)S(1)}, f32[67,256]{1,0:T(8,128)S(1)}, u32[]{:S(2)}, u32[]{:S(2)}) collective-permute-start(f32[67,256]{1,0:T(8,128)S(1)} %get-tuple-element.82), channel_id=1, source_target_pairs={{1,0},{2,1},{3,2},{4,3},{5,4},{6,5},{7,6},{8,7},{9,8},{10,9},{11,1... | collective-permute-start | bytes 205832 | tf_op jit(solution)/shard_map/ppermute | solution.py:18
  68.0 36.9 %collective-permute-done = f32[67,256]{1,0:T(8,128)S(1)} collective-permute-done((f32[67,256]{1,0:T(8,128)S(1)}, f32[67,256]{1,0:T(8,128)S(1)}, u32[]{:S(2)}, u32[]{:S(2)}) %collective-permute-start) | collective-permute-done | bytes 68640 | tf_op jit(solution)/shard_map/ppermute | solution.py:15
  105.0 11.9 %while.20 = (s32[]{:T(128)}, f32[4,64,256]{2,1,0:T(8,128)S(1)}, s32[4]{0:T(128)S(1)}, f32[67,1536]{1,0:T(8,128)S(1)}, s32[]{:T(128)}, /*index=5*/s32[1]{0:T(128)...) while((s32[]{:T(128)}, f32[4,64,256]{2,1,0:T(8,128)S(1)}, ...), condition=%wide.region_1.2_spmd, body=%wide.region_0.1_spmd.sunk | while | flops 152961040 | bytes 339289 | solution.py:82
  117.0 32.6 %all-gather.3.cloned.1.call-done = f32[128,64,64]{2,1,0:T(8,128)} async-done(((f32[1,64,64]{2,1,0:T(8,128)}), f32[128,64,64]{2,1,0:T(8,128)}) %all-gather.3.cloned.1.call-update) | async-done | bytes 2097168 | tf_op jit(solution)/shard_map/all_gather | solution.py:89
  149.6 5.3 %constant_dynamic-slice_fusion.3 = f32[128,64,16]{2,1,0:T(8,128)} fusion(f32[128,64,64]{2,1,0:T(8,128)} %all-gather.3.cloned.1.call-done, s32[]{:T(128)S(6)} %select_n.38), kind=kLoop, calls=%fused_computation.99 | loop fusion | bytes 1048580 | tf_op jit(solution)/shard_map/dynamic_slice | solution.py:88
  154.9 4.0 %copy.41 = f32[128,64,16]{0,1,2:T(8,128)S(1)} copy(f32[128,64,16]{2,1,0:T(8,128)} %constant_dynamic-slice_fusion.3) | data formatting | bytes 1048576
  159.5 17.6 %psum.29 = f32[64,64]{1,0:T(8,128)} all-reduce(f32[64,64]{1,0:T(8,128)S(1)} %convolution_bitcast_fusion.8), channel_id=1, replica_groups=mesh['leaf'=128,'sub'=4] {'sub'}, use_global_device_ids=true, to_apply=%region_3.4 | all-reduce | flops 4096 | bytes 32768 | tf_op jit(solution)/shard_map/psum | solution.py:92
  177.1 5.6 %copy.29 = f32[128,1,4096]{0,2,1:T(8,128)} copy(f32[128,1,4096]{2,1,0:T(1,128)} %all-to-all-done) | data formatting | bytes 4194304 | tf_op jit(solution)/shard_map/all_to_all | solution.py:63
  182.8 5.6 %copy.30 = f32[128,64,64]{2,1,0:T(8,128)} copy(f32[128,64,64]{0,2,1:T(8,128)} %bitcast.123) | data formatting | bytes 4194304 | tf_op jit(solution)/shard_map/reshape | solution.py:36
  188.4 2.9 gather_fusion.1
  196.4 15.0 %psum.30 = f32[1,64,64]{2,1,0:T(8,128)} all-reduce(f32[1,64,64]{2,1,0:T(8,128)S(1)} %convolution_bitcast_fusion.7), channel_id=1, replica_groups=mesh['leaf'=128,'sub'=4] {'sub'}, use_global_device_ids=true, to_apply=%region_6.7 | all-reduce | flops 4096 | bytes 32768 | tf_op jit(solution)/shard_map/psum | solution.py:86
  211.4 2.9 gather_fusion.3
  214.4 4.7 %copy.33 = f32[128,64,64]{0,2,1:T(8,128)} copy(f32[128,64,64]{2,1,0:T(8,128)} %gather_fusion.3) | data formatting | bytes 4194304 | tf_op jit(solution)/shard_map/gather | solution.py:60
  219.1 5.7 %copy.34 = f32[128,1,4096]{2,1,0:T(1,128)} copy(f32[128,1,4096]{0,2,1:T(8,128)} %bitcast.124) | data formatting | bytes 4194304 | tf_op jit(solution)/shard_map/all_to_all | solution.py:63
  224.8 10.4 %all-to-all-start.1 = ((f32[128,1,4096]{2,1,0:T(1,128)}), f32[128,1,4096]{2,1,0:T(1,128)}, u32[]{:S(2)}, u32[]{:S(2)}) async-start(f32[128,1,4096]{2,1,0:T(1,128)} %copy.34), calls=%async_computation.1 | async-start | bytes 4194304 | tf_op jit(solution)/shard_map/all_to_all | solution.py:63
  235.4 2.6 collective-permute-start.2
  238.0 7.2 %collective-permute-start.3 = (f32[67,256]{1,0:T(8,128)S(1)}, f32[67,256]{1,0:T(8,128)S(1)}, u32[]{:S(2)}, u32[]{:S(2)}) collective-permute-start(f32[67,256]{1,0:T(8,128)S(1)} %get-tuple-element.80), channel_id=1, source_target_pairs={{1,0},{2,1},{3,2},{4,3},{5,4},{6,5},{7,6},{8,7},{9,8},{10,9},{11,1... | collective-permute-start | bytes 205832 | tf_op jit(solution)/shard_map/ppermute | solution.py:18
  245.1 40.4 %collective-permute-done.2 = f32[67,256]{1,0:T(8,128)S(1)} collective-permute-done((f32[67,256]{1,0:T(8,128)S(1)}, f32[67,256]{1,0:T(8,128)S(1)}, u32[]{:S(2)}, u32[]{:S(2)}) %collective-permute-start.2) | collective-permute-done | bytes 68640 | tf_op jit(solution)/shard_map/ppermute | solution.py:15
  285.6 11.9 %while.21 = (s32[]{:T(128)}, f32[4,64,256]{2,1,0:T(8,128)S(1)}, s32[4]{0:T(128)S(1)}, f32[67,1536]{1,0:T(8,128)S(1)}, s32[]{:T(128)}, /*index=5*/s32[1]{0:T(128)...) while((s32[]{:T(128)}, f32[4,64,256]{2,1,0:T(8,128)S(1)}, ...), condition=%wide.region_5.6_spmd, body=%wide.region_4.5_spmd.sunk | while | flops 152961040 | bytes 339289 | solution.py:82
  297.6 29.0 %all-gather.5.cloned.1.call-done = f32[128,64,64]{2,1,0:T(8,128)} async-done(((f32[1,64,64]{2,1,0:T(8,128)}), f32[128,64,64]{2,1,0:T(8,128)}) %all-gather.5.cloned.1.call-update) | async-done | bytes 2097168 | tf_op jit(solution)/shard_map/all_gather | solution.py:89
  326.5 5.3 %constant_dynamic-slice_fusion.2 = f32[128,64,16]{2,1,0:T(8,128)} fusion(f32[128,64,64]{2,1,0:T(8,128)} %all-gather.5.cloned.1.call-done, s32[]{:T(128)S(6)} %select_n.38), kind=kLoop, calls=%fused_computation.98 | loop fusion | bytes 1048580 | tf_op jit(solution)/shard_map/dynamic_slice | solution.py:88
  331.8 4.0 %copy.42 = f32[128,64,16]{0,1,2:T(8,128)S(1)} copy(f32[128,64,16]{2,1,0:T(8,128)} %constant_dynamic-slice_fusion.2) | data formatting | bytes 1048576
  336.4 17.6 %psum.31 = f32[64,64]{1,0:T(8,128)} all-reduce(f32[64,64]{1,0:T(8,128)S(1)} %convolution_bitcast_fusion.6), channel_id=1, replica_groups=mesh['leaf'=128,'sub'=4] {'sub'}, use_global_device_ids=true, to_apply=%region_7.8 | all-reduce | flops 4096 | bytes 32768 | tf_op jit(solution)/shard_map/psum | solution.py:92
  354.0 5.6 %copy.35 = f32[128,1,4096]{0,2,1:T(8,128)} copy(f32[128,1,4096]{2,1,0:T(1,128)} %all-to-all-done.1) | data formatting | bytes 4194304 | tf_op jit(solution)/shard_map/all_to_all | solution.py:63
  359.7 5.6 %copy.36 = f32[128,64,64]{2,1,0:T(8,128)} copy(f32[128,64,64]{0,2,1:T(8,128)} %bitcast.125) | data formatting | bytes 4194304 | tf_op jit(solution)/shard_map/reshape | solution.py:36
  365.3 2.8 gather_fusion.4
  (114 shorter events, 29.6 us)
Async XLA Ops:
  6.5 60.9 %copy-start = (f32[32,64,64]{2,1,0:T(8,128)S(1)}, f32[32,64,64]{2,1,0:T(8,128)}, u32[]{:S(2)}) copy-start(f32[32,64,64]{2,1,0:T(8,128)} %param.19) | copy-start | bytes 1572868
  6.5 143.1 %all-gather.3.cloned.1.call-start = ((), (), s32[]{:S(2)}) async-start(), calls=%async_computation.2 | async-start | bytes 4227072 | tf_op jit(solution)/shard_map/all_gather | solution.py:89
  27.6 0.6 copy-start.12
  34.8 22.0 %copy-start.7 = (f32[64,1024]{1,0:T(8,128)S(1)}, f32[64,1024]{1,0:T(8,128)}, u32[]{:S(2)}) copy-start(f32[64,1024]{1,0:T(8,128)} %param.14) | copy-start | bytes 786436
  34.8 22.0 %copy-start.10 = (f32[3,1024]{1,0:T(4,128)S(1)}, f32[3,1024]{1,0:T(4,128)}, u32[]{:S(2)}) copy-start(f32[3,1024]{1,0:T(4,128)} %param.15) | copy-start | bytes 36868
  34.8 31.8 %copy-start.13 = (s32[4,8]{1,0:T(4,128)S(1)}, s32[4,8]{1,0:T(4,128)}, u32[]{:S(2)}) copy-start(s32[4,8]{1,0:T(4,128)} %param.22) | copy-start | bytes 388
  34.8 31.9 %copy-start.14 = (s32[4,8]{1,0:T(4,128)S(1)}, s32[4,8]{1,0:T(4,128)}, u32[]{:S(2)}) copy-start(s32[4,8]{1,0:T(4,128)} %param.23) | copy-start | bytes 388
  38.9 138.2 %all-to-all-start = ((f32[128,1,4096]{2,1,0:T(1,128)}), f32[128,1,4096]{2,1,0:T(1,128)}, u32[]{:S(2)}, u32[]{:S(2)}) async-start(f32[128,1,4096]{2,1,0:T(1,128)} %copy.28), calls=%async_computation | async-start | bytes 4194304 | tf_op jit(solution)/shard_map/all_to_all | solution.py:63
  56.7 269.8 %all-gather.5.cloned.1.call-start = ((), (), s32[]{:S(2)}) async-start(), calls=%async_computation.3 | async-start | bytes 4227072 | tf_op jit(solution)/shard_map/all_gather | solution.py:89
  56.8 48.1 %collective-permute-start = (f32[67,256]{1,0:T(8,128)S(1)}, f32[67,256]{1,0:T(8,128)S(1)}, u32[]{:S(2)}, u32[]{:S(2)}) collective-permute-start(f32[67,256]{1,0:T(8,128)S(1)} %get-tuple-element.81), channel_id=1, source_target_pairs={{0,1},{1,2},{2,3},{3,4},{4,5},{5,6},{6,7},{7,8},{8,9},{9,10},{10,1... | collective-permute-start | bytes 205832 | tf_op jit(solution)/shard_map/ppermute | solution.py:15
  58.8 46.2 %collective-permute-start.1 = (f32[67,256]{1,0:T(8,128)S(1)}, f32[67,256]{1,0:T(8,128)S(1)}, u32[]{:S(2)}, u32[]{:S(2)}) collective-permute-start(f32[67,256]{1,0:T(8,128)S(1)} %get-tuple-element.82), channel_id=1, source_target_pairs={{1,0},{2,1},{3,2},{4,3},{5,4},{6,5},{7,6},{8,7},{9,8},{10,9},{11,1... | collective-permute-start | bytes 205832 | tf_op jit(solution)/shard_map/ppermute | solution.py:18
  117.0 37.9 %copy-start.2 = (f32[4,64,256]{2,1,0:T(8,128)}, f32[4,64,256]{2,1,0:T(8,128)S(1)}, u32[]{:S(2)}) copy-start(f32[4,64,256]{2,1,0:T(8,128)S(1)} %get-tuple-element.49) | copy-start | bytes 786436
  154.9 4.0 %copy-start.4 = (f32[1,128,16,64]{1,3,2,0:T(8,128)S(1)}, f32[1,128,16,64]{1,3,2,0:T(8,128)}, u32[]{:S(2)}) copy-start(f32[1,128,16,64]{1,3,2,0:T(8,128)} %param.20) | copy-start | bytes 1572868
  182.8 9.7 %copy-start.8 = (f32[4,64,64]{2,1,0:T(8,128)S(1)}, f32[4,64,64]{2,1,0:T(8,128)}, u32[]{:S(2)}) copy-start(f32[4,64,64]{2,1,0:T(8,128)} %param.18) | copy-start | bytes 196612
  182.8 10.7 %copy-start.1 = (f32[4,64,256]{2,1,0:T(8,128)S(1)}, f32[4,64,256]{2,1,0:T(8,128)}, u32[]{:S(2)}) copy-start(f32[4,64,256]{2,1,0:T(8,128)} %param.16) | copy-start | bytes 786436
  219.1 16.1 %copy-start.3 = (f32[4,64,256]{2,1,0:T(8,128)S(1)}, f32[4,64,256]{2,1,0:T(8,128)}, u32[]{:S(2)}) copy-start(f32[4,64,256]{2,1,0:T(8,128)} %copy-done.2) | copy-start | bytes 786436
  224.8 129.2 %all-to-all-start.1 = ((f32[128,1,4096]{2,1,0:T(1,128)}), f32[128,1,4096]{2,1,0:T(1,128)}, u32[]{:S(2)}, u32[]{:S(2)}) async-start(f32[128,1,4096]{2,1,0:T(1,128)} %copy.34), calls=%async_computation.1 | async-start | bytes 4194304 | tf_op jit(solution)/shard_map/all_to_all | solution.py:63
  235.4 50.2 %collective-permute-start.2 = (f32[67,256]{1,0:T(8,128)S(1)}, f32[67,256]{1,0:T(8,128)S(1)}, u32[]{:S(2)}, u32[]{:S(2)}) collective-permute-start(f32[67,256]{1,0:T(8,128)S(1)} %get-tuple-element.79), channel_id=1, source_target_pairs={{0,1},{1,2},{2,3},{3,4},{4,5},{5,6},{6,7},{7,8},{8,9},{9,10},{10,1... | collective-permute-start | bytes 205832 | tf_op jit(solution)/shard_map/ppermute | solution.py:15
  238.0 47.6 %collective-permute-start.3 = (f32[67,256]{1,0:T(8,128)S(1)}, f32[67,256]{1,0:T(8,128)S(1)}, u32[]{:S(2)}, u32[]{:S(2)}) collective-permute-start(f32[67,256]{1,0:T(8,128)S(1)} %get-tuple-element.80), channel_id=1, source_target_pairs={{1,0},{2,1},{3,2},{4,3},{5,4},{6,5},{7,6},{8,7},{9,8},{10,9},{11,1... | collective-permute-start | bytes 205832 | tf_op jit(solution)/shard_map/ppermute | solution.py:18
  297.5 29.0 %copy-start.6 = (f32[4,64,256]{2,1,0:T(8,128)}, f32[4,64,256]{2,1,0:T(8,128)S(1)}, u32[]{:S(2)}) copy-start(f32[4,64,256]{2,1,0:T(8,128)S(1)} %get-tuple-element.50) | copy-start | bytes 786436
  331.8 4.0 %copy-start.5 = (f32[1,128,16,64]{1,3,2,0:T(8,128)S(1)}, f32[1,128,16,64]{1,3,2,0:T(8,128)}, u32[]{:S(2)}) copy-start(f32[1,128,16,64]{1,3,2,0:T(8,128)} %param.20) | copy-start | bytes 1572868
  359.7 5.6 %copy-start.11 = (s32[1024]{0:T(1024)S(1)}, s32[1024]{0:T(1024)}, u32[]{:S(2)}) copy-start(s32[1024]{0:T(1024)} %get-tuple-element.84) | copy-start | bytes 12292
  359.7 9.5 %copy-start.9 = (f32[4,64,64]{2,1,0:T(8,128)S(1)}, f32[4,64,64]{2,1,0:T(8,128)}, u32[]{:S(2)}) copy-start(f32[4,64,64]{2,1,0:T(8,128)} %param.18) | copy-start | bytes 196612
Sparse Core Ops, SparseCore 0:
  27.1 122.4 all-gather.2
  211.6 114.9 all-gather.4
where the time goes:
time: 381 us; the launch traced here: 379 us
  waiting for transfers between devices  139 us (36%)
  local copies, waits for them, and re-layouts  79.5 us (21%)
  blocking collectives  67.9 us (18%)
  starting transfers between devices  47.8 us (13%)
  matrix products  18.6 us (5%)
  between operations  13.8 us (4%)
  loops' own time  10.3 us (3%)
    ppermute x2, waiting for transfers between devices, extended(): lax.ppermute(lax.slice_in_dim(block, block.shape[dim] - width, None, axis...  77.3 us
    all_gather x2, waiting for transfers between devices, one_product(): lax.all_gather(parent[None], 'leaf', axis=0, tiled=True)  61.6 us
    psum x2, blocking collectives, one_product(): top_term = lax.psum(top_partial, 'sub')  35.2 us
    psum x2, blocking collectives, one_product(): parent = lax.psum(parent_part, 'sub')  32.7 us
    all_to_all x2, starting transfers between devices, one_product(): lax.all_to_all(outgoing.reshape(slot_total, rhs_count * rank), 'leaf', sp...  28.2 us
    all_to_all x4, local copies, waits for them, and re-layouts, one_product(): lax.all_to_all(outgoing.reshape(slot_total, rhs_count * rank), 'leaf', sp...  21 us
    ppermute x2, starting transfers between devices, extended(): lax.ppermute(lax.slice_in_dim(block, 0, width, axis=dim), axis, backward)  15 us
    gather x4, local copies, waits for them, and re-layouts, one_product(): outgoing = skeleton[send_leaf.reshape(-1)]  14.2 us
  transfers between devices with their start and end apart: 8, of which 4 were waited for; matrix products, arithmetic and copies ran while one was open for 16% of the time, Pallas kernels for 0%

commit v1 on v0

--- a/solution.py
+++ b/solution.py
@@ -86,7 +86,12 @@
     parent = lax.psum(parent_part, "sub")
     row_start = lax.axis_index("sub") * quarter
     rows = lax.dynamic_slice_in_dim(
-        lax.all_gather(parent[None], "leaf", axis=0, tiled=True), row_start, quarter, 2
+        jnp.concatenate(
+            lax.all_to_all(jnp.stack([parent[None]] * lax.axis_size("leaf")), "leaf", 0, 0), axis=0
+        ),
+        row_start,
+        quarter,
+        2,
     )
     top_partial = add_top(rows, coupling_rows)
     top_term = lax.psum(top_partial, "sub")

time: 381 us -> 428 us (1.12)
  the two profiles are of different devices: /device:TPU:16 before, /device:TPU:48 now
where the time goes in v1:
time: 428 us; the launch traced here: 420 us
  waiting for transfers between devices  151 us (35%)
  local copies, waits for them, and re-layouts  90.7 us (21%)
  starting transfers between devices  69.1 us (16%)
  blocking collectives  63 us (15%)
  other arithmetic  19 us (4%)
  matrix products  16 us (4%)
  loops' own time  11.1 us (3%)
    ppermute x2, waiting for transfers between devices, extended(): lax.ppermute(lax.slice_in_dim(block, block.shape[dim] - width, None, axis...  76.2 us
    all_to_all x2, waiting for transfers between devices, one_product(): lax.all_to_all(jnp.stack([parent[None]] * lax.axis_size('leaf')), 'leaf',...  74.7 us
    psum x2, blocking collectives, one_product(): parent = lax.psum(parent_part, 'sub')  33.4 us
    psum x2, blocking collectives, one_product(): top_term = lax.psum(top_partial, 'sub')  29.6 us
    all_to_all x2, starting transfers between devices, one_product(): lax.all_to_all(jnp.stack([parent[None]] * lax.axis_size('leaf')), 'leaf',...  28.1 us
    unnamed x40, local copies, waits for them, and re-layouts  26 us
    all_to_all x4, local copies, waits for them, and re-layouts, one_product(): lax.all_to_all(outgoing.reshape(slot_total, rhs_count * rank), 'leaf', sp...  21 us
    all_to_all x2, starting transfers between devices, one_product(): lax.all_to_all(outgoing.reshape(slot_total, rhs_count * rank), 'leaf', sp...  20.7 us
  transfers between devices with their start and end apart: 8, of which 4 were waited for; matrix products, arithmetic and copies ran while one was open for 17% of the time, Pallas kernels for 0%

profile of v1, /device:TPU:48, one launch (start us, length us, event | category | flops | bytes accessed | tf_op | source)
XLA Modules:
  0.0 420.5 jit_solution(2232198041076904299)
XLA Ops:
  2.7 17.1 %psum.28 = f32[64,64]{1,0:T(8,128)S(1)} all-reduce(f32[64,64]{1,0:T(8,128)S(1)} %convolution_bitcast_fusion.9), channel_id=1, replica_groups=mesh['leaf'=128,'sub'=4] {'sub'}, use_global_device_ids=true, to_apply=%region_2.3 | all-reduce | flops 4096 | bytes 32768 | tf_op jit(solution)/shard_map/psum | solution.py:86
  22.3 5.5 %reshape.149 = f32[128,1,4096]{2,1,0:T(1,128)} reshape(f32[128,1,64,64]{3,2,1,0:T(8,128)} %broadcast_bitcast_fusion.1) | data formatting | bytes 4194304
  27.9 17.8 %all-to-all-start.1 = ((f32[128,1,4096]{2,1,0:T(1,128)}), f32[128,1,4096]{2,1,0:T(1,128)}, u32[]{:S(2)}, u32[]{:S(2)}) async-start(f32[128,1,4096]{2,1,0:T(1,128)} %reshape.149), calls=%async_computation.1 | async-start | bytes 4194304 | tf_op jit(solution)/shard_map/all_to_all | solution.py:90
  49.1 3.8 copy.27
  52.9 4.0 copy.28
  56.9 38.4 %all-to-all-done.1 = f32[128,1,4096]{2,1,0:T(1,128)} async-done(((f32[128,1,4096]{2,1,0:T(1,128)}), f32[128,1,4096]{2,1,0:T(1,128)}, u32[]{:S(2)}, u32[]{:S(2)}) %all-to-all-start.1) | async-done | bytes 2097184 | tf_op jit(solution)/shard_map/all_to_all | solution.py:90
  95.3 10.4 %all-to-all-start = ((f32[128,1,4096]{2,1,0:T(1,128)}), f32[128,1,4096]{2,1,0:T(1,128)}, u32[]{:S(2)}, u32[]{:S(2)}) async-start(f32[128,1,4096]{2,1,0:T(1,128)} %copy.28), calls=%async_computation | async-start | bytes 4194304 | tf_op jit(solution)/shard_map/all_to_all | solution.py:63
  107.7 8.3 %collective-permute-start.1 = (f32[67,256]{1,0:T(8,128)S(1)}, f32[67,256]{1,0:T(8,128)S(1)}, u32[]{:S(2)}, u32[]{:S(2)}) collective-permute-start(f32[67,256]{1,0:T(8,128)S(1)} %get-tuple-element.82), channel_id=1, source_target_pairs={{1,0},{2,1},{3,2},{4,3},{5,4},{6,5},{7,6},{8,7},{9,8},{10,9},{11,1... | collective-permute-start | bytes 205832 | tf_op jit(solution)/shard_map/ppermute | solution.py:18
  117.5 37.1 %collective-permute-done = f32[67,256]{1,0:T(8,128)S(1)} collective-permute-done((f32[67,256]{1,0:T(8,128)S(1)}, f32[67,256]{1,0:T(8,128)S(1)}, u32[]{:S(2)}, u32[]{:S(2)}) %collective-permute-start) | collective-permute-done | bytes 68640 | tf_op jit(solution)/shard_map/ppermute | solution.py:15
  154.7 12.5 %while.20 = (s32[]{:T(128)}, f32[4,64,256]{2,1,0:T(8,128)S(1)}, s32[4]{0:T(128)S(1)}, f32[67,1536]{1,0:T(8,128)S(1)}, s32[]{:T(128)}, /*index=5*/s32[1]{0:T(128)...) while((s32[]{:T(128)}, f32[4,64,256]{2,1,0:T(8,128)S(1)}, ...), condition=%wide.region_1.2_spmd, body=%wide.region_0.1_spmd.sunk | while | flops 152961040 | bytes 339289 | solution.py:82
  167.8 8.7 %reduce.12 = f32[128,4096]{1,0:T(8,128)} reduce(f32[128,1,4096]{2,1,0:T(1,128)} %all-to-all-done.1, f32[]{:T(128)} %broadcast.98), dimensions={1}, to_apply=%all_to_all.20.reduce_sub_computation | reduce | bytes 4194308 | tf_op jit(solution)/shard_map/all_to_all | solution.py:90
  176.5 4.7 %reshape.150 = f32[128,1,64,64]{3,2,1,0:T(8,128)} reshape(f32[128,4096]{1,0:T(8,128)} %reduce.12) | data formatting | bytes 4194304
  183.5 14.6 %psum.29 = f32[64,64]{1,0:T(8,128)S(1)} all-reduce(f32[64,64]{1,0:T(8,128)S(1)} %convolution_bitcast_fusion.8), channel_id=1, replica_groups=mesh['leaf'=128,'sub'=4] {'sub'}, use_global_device_ids=true, to_apply=%region_3.4 | all-reduce | flops 4096 | bytes 32768 | tf_op jit(solution)/shard_map/psum | solution.py:97
  198.1 5.7 %copy.29 = f32[128,1,4096]{0,2,1:T(8,128)} copy(f32[128,1,4096]{2,1,0:T(1,128)} %all-to-all-done) | data formatting | bytes 4194304 | tf_op jit(solution)/shard_map/all_to_all | solution.py:63
  203.8 5.6 %copy.30 = f32[128,64,64]{2,1,0:T(8,128)} copy(f32[128,64,64]{0,2,1:T(8,128)} %bitcast.131) | data formatting | bytes 4194304 | tf_op jit(solution)/shard_map/reshape | solution.py:36
  209.4 2.8 gather_fusion.1
  214.7 16.3 %psum.30 = f32[64,64]{1,0:T(8,128)S(1)} all-reduce(f32[64,64]{1,0:T(8,128)S(1)} %convolution_bitcast_fusion.7), channel_id=1, replica_groups=mesh['leaf'=128,'sub'=4] {'sub'}, use_global_device_ids=true, to_apply=%region_6.7 | all-reduce | flops 4096 | bytes 32768 | tf_op jit(solution)/shard_map/psum | solution.py:86
  233.5 5.5 %reshape.151 = f32[128,1,4096]{2,1,0:T(1,128)} reshape(f32[128,1,64,64]{3,2,1,0:T(8,128)} %broadcast_bitcast_fusion) | data formatting | bytes 4194304
  239.1 10.3 %all-to-all-start.3 = ((f32[128,1,4096]{2,1,0:T(1,128)}), f32[128,1,4096]{2,1,0:T(1,128)}, u32[]{:S(2)}, u32[]{:S(2)}) async-start(f32[128,1,4096]{2,1,0:T(1,128)} %reshape.151), calls=%async_computation.3 | async-start | bytes 4194304 | tf_op jit(solution)/shard_map/all_to_all | solution.py:90
  249.4 2.9 gather_fusion.3
  252.3 4.8 %copy.34 = f32[128,64,64]{0,2,1:T(8,128)} copy(f32[128,64,64]{2,1,0:T(8,128)} %gather_fusion.3) | data formatting | bytes 4194304 | tf_op jit(solution)/shard_map/gather | solution.py:60
  257.0 5.7 %copy.35 = f32[128,1,4096]{2,1,0:T(1,128)} copy(f32[128,1,4096]{0,2,1:T(8,128)} %bitcast.132) | data formatting | bytes 4194304 | tf_op jit(solution)/shard_map/all_to_all | solution.py:63
  262.7 36.4 %all-to-all-done.3 = f32[128,1,4096]{2,1,0:T(1,128)} async-done(((f32[128,1,4096]{2,1,0:T(1,128)}), f32[128,1,4096]{2,1,0:T(1,128)}, u32[]{:S(2)}, u32[]{:S(2)}) %all-to-all-start.3) | async-done | bytes 2097184 | tf_op jit(solution)/shard_map/all_to_all | solution.py:90
  299.0 10.4 %all-to-all-start.2 = ((f32[128,1,4096]{2,1,0:T(1,128)}), f32[128,1,4096]{2,1,0:T(1,128)}, u32[]{:S(2)}, u32[]{:S(2)}) async-start(f32[128,1,4096]{2,1,0:T(1,128)} %copy.35), calls=%async_computation.2 | async-start | bytes 4194304 | tf_op jit(solution)/shard_map/all_to_all | solution.py:63
  311.5 8.1 %collective-permute-start.3 = (f32[67,256]{1,0:T(8,128)S(1)}, f32[67,256]{1,0:T(8,128)S(1)}, u32[]{:S(2)}, u32[]{:S(2)}) collective-permute-start(f32[67,256]{1,0:T(8,128)S(1)} %get-tuple-element.80), channel_id=1, source_target_pairs={{1,0},{2,1},{3,2},{4,3},{5,4},{6,5},{7,6},{8,7},{9,8},{10,9},{11,1... | collective-permute-start | bytes 205832 | tf_op jit(solution)/shard_map/ppermute | solution.py:18
  319.6 39.0 %collective-permute-done.2 = f32[67,256]{1,0:T(8,128)S(1)} collective-permute-done((f32[67,256]{1,0:T(8,128)S(1)}, f32[67,256]{1,0:T(8,128)S(1)}, u32[]{:S(2)}, u32[]{:S(2)}) %collective-permute-start.2) | collective-permute-done | bytes 68640 | tf_op jit(solution)/shard_map/ppermute | solution.py:15
  358.7 12.5 %while.21 = (s32[]{:T(128)}, f32[4,64,256]{2,1,0:T(8,128)S(1)}, s32[4]{0:T(128)S(1)}, f32[67,1536]{1,0:T(8,128)S(1)}, s32[]{:T(128)}, /*index=5*/s32[1]{0:T(128)...) while((s32[]{:T(128)}, f32[4,64,256]{2,1,0:T(8,128)S(1)}, ...), condition=%wide.region_5.6_spmd, body=%wide.region_4.5_spmd.sunk | while | flops 152961040 | bytes 339289 | solution.py:82
  371.2 8.7 %reduce.13 = f32[128,4096]{1,0:T(8,128)} reduce(f32[128,1,4096]{2,1,0:T(1,128)} %all-to-all-done.3, f32[]{:T(128)} %broadcast.98), dimensions={1}, to_apply=%all_to_all.23.reduce_sub_computation | reduce | bytes 4194308 | tf_op jit(solution)/shard_map/all_to_all | solution.py:90
  379.9 4.7 %reshape.152 = f32[128,1,64,64]{3,2,1,0:T(8,128)} reshape(f32[128,4096]{1,0:T(8,128)} %reduce.13) | data formatting | bytes 4194304
  386.9 15.0 %psum.31 = f32[64,64]{1,0:T(8,128)} all-reduce(f32[64,64]{1,0:T(8,128)S(1)} %convolution_bitcast_fusion.6), channel_id=1, replica_groups=mesh['leaf'=128,'sub'=4] {'sub'}, use_global_device_ids=true, to_apply=%region_7.8 | all-reduce | flops 4096 | bytes 32768 | tf_op jit(solution)/shard_map/psum | solution.py:97
  401.9 5.6 %copy.36 = f32[128,1,4096]{0,2,1:T(8,128)} copy(f32[128,1,4096]{2,1,0:T(1,128)} %all-to-all-done.2) | data formatting | bytes 4194304 | tf_op jit(solution)/shard_map/all_to_all | solution.py:63
  407.5 5.7 %copy.37 = f32[128,64,64]{2,1,0:T(8,128)} copy(f32[128,64,64]{0,2,1:T(8,128)} %bitcast.133) | data formatting | bytes 4194304 | tf_op jit(solution)/shard_map/reshape | solution.py:36
  (125 shorter events, 45.2 us)
Async XLA Ops:
  0.0 116.9 %copy-start = (f32[32,64,64]{2,1,0:T(8,128)S(1)}, f32[32,64,64]{2,1,0:T(8,128)}, u32[]{:S(2)}) copy-start(f32[32,64,64]{2,1,0:T(8,128)} %param.19) | copy-start | bytes 1572868
  22.3 23.3 %copy-start.15 = (s32[1,1,128,1]{2,3,1,0:T(1,128)S(1)}, s32[1,1,128,1]{2,3,1,0:T(1,128)}, u32[]{:S(2)}) copy-start(s32[1,1,128,1]{2,3,1,0:T(1,128)} %param.21) | copy-start | bytes 1540
  27.9 67.5 %all-to-all-start.1 = ((f32[128,1,4096]{2,1,0:T(1,128)}), f32[128,1,4096]{2,1,0:T(1,128)}, u32[]{:S(2)}, u32[]{:S(2)}) async-start(f32[128,1,4096]{2,1,0:T(1,128)} %reshape.149), calls=%async_computation.1 | async-start | bytes 4194304 | tf_op jit(solution)/shard_map/all_to_all | solution.py:90
  45.7 0.6 copy-start.12
  52.9 52.9 %copy-start.6 = (f32[64,1024]{1,0:T(8,128)S(1)}, f32[64,1024]{1,0:T(8,128)}, u32[]{:S(2)}) copy-start(f32[64,1024]{1,0:T(8,128)} %param.14) | copy-start | bytes 786436
  52.9 52.9 %copy-start.9 = (f32[3,1024]{1,0:T(4,128)S(1)}, f32[3,1024]{1,0:T(4,128)}, u32[]{:S(2)}) copy-start(f32[3,1024]{1,0:T(4,128)} %param.15) | copy-start | bytes 36868
  52.9 63.2 %copy-start.13 = (s32[4,8]{1,0:T(4,128)S(1)}, s32[4,8]{1,0:T(4,128)}, u32[]{:S(2)}) copy-start(s32[4,8]{1,0:T(4,128)} %param.23) | copy-start | bytes 388
  52.9 63.3 %copy-start.14 = (s32[4,8]{1,0:T(4,128)S(1)}, s32[4,8]{1,0:T(4,128)}, u32[]{:S(2)}) copy-start(s32[4,8]{1,0:T(4,128)} %param.22) | copy-start | bytes 388
  95.3 102.7 %all-to-all-start = ((f32[128,1,4096]{2,1,0:T(1,128)}), f32[128,1,4096]{2,1,0:T(1,128)}, u32[]{:S(2)}, u32[]{:S(2)}) async-start(f32[128,1,4096]{2,1,0:T(1,128)} %copy.28), calls=%async_computation | async-start | bytes 4194304 | tf_op jit(solution)/shard_map/all_to_all | solution.py:63
  105.8 48.8 %collective-permute-start = (f32[67,256]{1,0:T(8,128)S(1)}, f32[67,256]{1,0:T(8,128)S(1)}, u32[]{:S(2)}, u32[]{:S(2)}) collective-permute-start(f32[67,256]{1,0:T(8,128)S(1)} %get-tuple-element.81), channel_id=1, source_target_pairs={{0,1},{1,2},{2,3},{3,4},{4,5},{5,6},{6,7},{7,8},{8,9},{9,10},{10,1... | collective-permute-start | bytes 205832 | tf_op jit(solution)/shard_map/ppermute | solution.py:15
  107.7 46.9 %collective-permute-start.1 = (f32[67,256]{1,0:T(8,128)S(1)}, f32[67,256]{1,0:T(8,128)S(1)}, u32[]{:S(2)}, u32[]{:S(2)}) collective-permute-start(f32[67,256]{1,0:T(8,128)S(1)} %get-tuple-element.82), channel_id=1, source_target_pairs={{1,0},{2,1},{3,2},{4,3},{5,4},{6,5},{7,6},{8,7},{9,8},{10,9},{11,1... | collective-permute-start | bytes 205832 | tf_op jit(solution)/shard_map/ppermute | solution.py:18
  176.5 6.4 %copy-start.3 = (f32[1,128,16,64]{1,3,2,0:T(8,128)S(1)}, f32[1,128,16,64]{1,3,2,0:T(8,128)}, u32[]{:S(2)}) copy-start(f32[1,128,16,64]{1,3,2,0:T(8,128)} %param.20) | copy-start | bytes 1572868
  203.7 5.6 %copy-start.10 = (s32[1024]{0:T(1024)S(1)}, s32[1024]{0:T(1024)}, u32[]{:S(2)}) copy-start(s32[1024]{0:T(1024)} %get-tuple-element.84) | copy-start | bytes 12292
  203.7 9.6 %copy-start.8 = (f32[4,64,64]{2,1,0:T(8,128)S(1)}, f32[4,64,64]{2,1,0:T(8,128)}, u32[]{:S(2)}) copy-start(f32[4,64,64]{2,1,0:T(8,128)} %param.18) | copy-start | bytes 196612
  203.8 9.9 %copy-start.2 = (f32[4,64,256]{2,1,0:T(8,128)S(1)}, f32[4,64,256]{2,1,0:T(8,128)}, u32[]{:S(2)}) copy-start(f32[4,64,256]{2,1,0:T(8,128)} %param.16) | copy-start | bytes 786436
  209.4 5.0 %copy-start.7 = (f32[4,64,64]{2,1,0:T(8,128)S(1)}, f32[4,64,64]{2,1,0:T(8,128)}, u32[]{:S(2)}) copy-start(f32[4,64,64]{2,1,0:T(8,128)} %param.17) | copy-start | bytes 196612
  239.1 60.0 %all-to-all-start.3 = ((f32[128,1,4096]{2,1,0:T(1,128)}), f32[128,1,4096]{2,1,0:T(1,128)}, u32[]{:S(2)}, u32[]{:S(2)}) async-start(f32[128,1,4096]{2,1,0:T(1,128)} %reshape.151), calls=%async_computation.3 | async-start | bytes 4194304 | tf_op jit(solution)/shard_map/all_to_all | solution.py:90
  299.0 102.9 %all-to-all-start.2 = ((f32[128,1,4096]{2,1,0:T(1,128)}), f32[128,1,4096]{2,1,0:T(1,128)}, u32[]{:S(2)}, u32[]{:S(2)}) async-start(f32[128,1,4096]{2,1,0:T(1,128)} %copy.35), calls=%async_computation.2 | async-start | bytes 4194304 | tf_op jit(solution)/shard_map/all_to_all | solution.py:63
  309.6 49.0 %collective-permute-start.2 = (f32[67,256]{1,0:T(8,128)S(1)}, f32[67,256]{1,0:T(8,128)S(1)}, u32[]{:S(2)}, u32[]{:S(2)}) collective-permute-start(f32[67,256]{1,0:T(8,128)S(1)} %get-tuple-element.79), channel_id=1, source_target_pairs={{0,1},{1,2},{2,3},{3,4},{4,5},{5,6},{6,7},{7,8},{8,9},{9,10},{10,1... | collective-permute-start | bytes 205832 | tf_op jit(solution)/shard_map/ppermute | solution.py:15
  311.5 47.1 %collective-permute-start.3 = (f32[67,256]{1,0:T(8,128)S(1)}, f32[67,256]{1,0:T(8,128)S(1)}, u32[]{:S(2)}, u32[]{:S(2)}) collective-permute-start(f32[67,256]{1,0:T(8,128)S(1)} %get-tuple-element.80), channel_id=1, source_target_pairs={{1,0},{2,1},{3,2},{4,3},{5,4},{6,5},{7,6},{8,7},{9,8},{10,9},{11,1... | collective-permute-start | bytes 205832 | tf_op jit(solution)/shard_map/ppermute | solution.py:18
  371.2 13.3 %copy-start.5 = (f32[4,64,256]{2,1,0:T(8,128)}, f32[4,64,256]{2,1,0:T(8,128)S(1)}, u32[]{:S(2)}) copy-start(f32[4,64,256]{2,1,0:T(8,128)S(1)} %get-tuple-element.50) | copy-start | bytes 786436
  379.9 6.4 %copy-start.4 = (f32[1,128,16,64]{1,3,2,0:T(8,128)S(1)}, f32[1,128,16,64]{1,3,2,0:T(8,128)}, u32[]{:S(2)}) copy-start(f32[1,128,16,64]{1,3,2,0:T(8,128)} %param.20) | copy-start | bytes 1572868
  407.5 5.7 %copy-start.11 = (s32[1024]{0:T(1024)S(1)}, s32[1024]{0:T(1024)}, u32[]{:S(2)}) copy-start(s32[1024]{0:T(1024)} %get-tuple-element.84) | copy-start | bytes 12292
  407.5 12.7 %copy-start.1 = (f32[32,64,64]{2,1,0:T(8,128)S(1)}, f32[32,64,64]{2,1,0:T(8,128)}, u32[]{:S(2)}) copy-start(f32[32,64,64]{2,1,0:T(8,128)} %param.19) | copy-start | bytes 1572868
